TPU v7x, 128 devices: a whole 4x4x4 slice. The times are simulated.
128 devices in a mesh: dp: 4 (over z), latent: 32 (over x, y, core).
Axes of the slice: x: 4, y: 4, z: 4, core: 2. Of those that a mesh axis runs over, the one named last changes fastest.
Arguments:
- acts: bfloat16 [640, 8192], P(('dp', 'latent')), may hold values from -6 to 6
- chat_len: int32 [128], P(('dp', 'latent')), may hold values from 1 to 5, as said below
- group_of: int32 [640, 1], P(('dp', 'latent')), may hold values from 0 to 4; in each aligned block of 5 rows (0 to 4, 5 to 9, ...) no two rows name the same one
- w_enc: bfloat16 [2, 4096, 16384], P(None, None, 'latent'), may hold values from -0.0625 to 0.0625
- b_enc: float32 [16384], P('latent'), may hold values from -3 to 3
- w_dec: bfloat16 [16384, 8192], P('latent'), may hold values from -0.046875 to 0.046875
- b_dec: float32 [2, 4096], replicated, may hold values from -3 to 3
Outputs:
- grad_enc: bfloat16 [2, 4096, 16384], P(None, 'dp', 'latent')
- grad_dec: bfloat16 [16384, 8192], P('latent', 'dp')
- loss: float32 [], replicated
Inputs may be any that keep to these rules, and one draw needn't show every extreme that they name: `chat_len`: the last serving shard harvests all 5 rows. `group_of`: among the 5 row slots of each serving shard every value 0 to 4 appears exactly once.
All inputs are finite; a program needn't handle non-finite values.
Results may differ from a plain program's by a relative error of at most 0.02.
Values may be sent and summed in bfloat16 or wider, within the bound.
No kernel may reach another device: no remote copies, remote signals or barrier semaphores. Data moves between devices by JAX's collectives and lax.ppermute only.
A program may use at most 128 MiB of HBM per device.

v0:
```python
import jax
import jax.numpy as jnp
from jax import lax
from jax.sharding import PartitionSpec as P

sparsity_weight = 1.0
loss_scale = 8.0
norm_eps = 1e-06


def shards(acts, chat_len, group_of, w_enc, b_enc, w_dec, b_dec):
    groups = lax.axis_size("dp")
    slots = acts.shape[0]
    width = acts.shape[1]
    half = width // 2
    local_latents = w_enc.shape[2]
    capacity = slots // (groups + 1)
    slot_ids = jnp.arange(slots, dtype=jnp.int32)
    alive = (slot_ids < chat_len[0]).astype(jnp.float32)
    order = jnp.argsort(group_of[:, 0], stable=True)[: groups * capacity]
    own_count = jnp.sum(alive[order])
    outgoing = acts[order].reshape(groups, capacity, width)
    out_mask = alive[order].reshape(groups, capacity).astype(jnp.bfloat16)
    received, recv_mask = (
        lax.all_to_all(outgoing, "dp", split_axis=0, concat_axis=0, tiled=True),
        lax.all_to_all(out_mask, "dp", split_axis=0, concat_axis=0, tiled=True),
    )
    member_rows, member_mask = (
        lax.all_gather(received, "latent", axis=0, tiled=True),
        lax.all_gather(recv_mask, "latent", axis=0, tiled=True),
    )
    xg = member_rows.reshape(-1, width)
    maskg = member_mask.reshape(-1).astype(jnp.float32)
    total_rows = xg.shape[0]
    share_rows = total_rows // lax.axis_size("latent")
    first_row = lax.axis_index("latent") * share_rows
    wenc_flat = w_enc.reshape(width, local_latents)
    squares_dec = jnp.square(w_dec.astype(jnp.float32))
    norm_base = jnp.sqrt(jnp.sum(squares_dec[:, :half], axis=1) + norm_eps)
    norm_inst = jnp.sqrt(jnp.sum(squares_dec[:, half:], axis=1) + norm_eps)
    norm_sum = norm_base + norm_inst
    column_ids = jnp.arange(width, dtype=jnp.int32)
    bias_row = b_dec.reshape(width)
    pre = jnp.dot(xg, wenc_flat, preferred_element_type=jnp.float32) + b_enc[None, :]
    act = jnp.maximum(pre, 0.0)
    feats = act * act
    feats16 = feats.astype(jnp.bfloat16)
    partial_value = jnp.dot(feats16, w_dec, preferred_element_type=jnp.float32)
    recon = lax.psum(partial_value.astype(jnp.bfloat16), "latent").astype(jnp.float32)
    err = (recon + bias_row[None, :] - xg.astype(jnp.float32)) * maskg[:, None]
    err16 = err.astype(jnp.bfloat16)
    err_share = lax.dynamic_slice_in_dim(err, first_row, share_rows, 0)
    square_sum = jnp.sum(err_share * err_share)
    feat_sum = jnp.sum(feats * maskg[:, None], axis=0)
    local_loss = square_sum + sparsity_weight * jnp.sum(feat_sum * norm_sum)
    dfeat = 2.0 * lax.dot_general(
        err16, w_dec, (((1,), (1,)), ((), ())), preferred_element_type=jnp.float32
    )
    dfeat = dfeat + sparsity_weight * maskg[:, None] * norm_sum[None, :]
    dpre16 = (dfeat * 2.0 * act).astype(jnp.bfloat16)
    enc_term = lax.dot_general(
        xg, dpre16, (((0,), (0,)), ((), ())), preferred_element_type=jnp.float32
    )
    enc_term = enc_term.reshape(2, half, local_latents)
    dec_term = 2.0 * lax.dot_general(
        feats16, err16, (((0,), (0,)), ((), ())), preferred_element_type=jnp.float32
    )
    scale = jnp.where(
        column_ids[None, :] < half, (feat_sum / norm_base)[:, None], (feat_sum / norm_inst)[:, None]
    )
    dec_term = dec_term + sparsity_weight * scale * w_dec.astype(jnp.float32)
    enc_total = lax.psum_scatter(
        enc_term.astype(jnp.bfloat16), "dp", scatter_dimension=1, tiled=True
    ).astype(jnp.float32)
    dec_total = lax.psum_scatter(
        dec_term.astype(jnp.bfloat16), "dp", scatter_dimension=1, tiled=True
    ).astype(jnp.float32)
    total, count = lax.psum((local_loss, own_count), ("dp", "latent"))
    factor = loss_scale / count
    grad_enc = (enc_total * factor).astype(jnp.bfloat16)
    grad_dec = (dec_total * factor).astype(jnp.bfloat16)
    loss = total / (count * width)
    return (grad_enc, grad_dec, loss)


def solution(mesh):
    return jax.shard_map(
        shards,
        mesh=mesh,
        in_specs=(
            P(("dp", "latent"), None),
            P(("dp", "latent")),
            P(("dp", "latent"), None),
            P(None, None, "latent"),
            P("latent"),
            P("latent", None),
            P(),
        ),
        out_specs=(P(None, "dp", "latent"), P("latent", "dp"), P()),
        check_vma=False,
    )
```

profile of v0, /device:TPU:1, one launch (start us, length us, event | category | flops | bytes accessed | tf_op | source)
XLA Modules:
  0.0 414.3 jit_solution(3964806186658669848)
XLA Ops:
  7.2 0.0 copy-start
  7.2 0.0 all-gather.3.cloned.1.call-start
  7.2 1.6 sort.17
  8.9 0.0 copy-done
  8.9 0.6 gather_fusion
  9.5 0.5 broadcast.57
  10.0 0.7 reduce.2
  10.7 0.1 reshape.95
  10.8 10.1 %all_to_all.14 = bf16[4,2,4096]{2,1,0:T(2,128)(2,1)S(1)} all-to-all(bf16[4,2,4096]{2,1,0:T(2,128)(2,1)S(1)} %reshape.95), channel_id=1, replica_groups=mesh['dp'=4,'latent'=32] {'dp'}, dimensions={0} | all-to-all | bytes 131072 | tf_op jit(solution)/shard_map/all_to_all | solution.py:25
  20.9 0.7 reshape.96
  21.6 0.0 all-gather.3.cloned.1.call-update
  22.3 0.6 gather_fusion.1
  23.0 0.6 fusion.25
  23.6 0.7 copy.17
  24.3 3.2 all-to-all-start.1
  27.5 0.0 all-reduce.4.cloned.1.call-start
  27.5 1.3 dynamic-slice
  29.6 1.9 all-to-all-done.1
  31.5 0.1 reduce.1
  31.6 0.2 dynamic-update-slice
  31.8 65.9 %all-reduce = bf16[128]{0:T(256)(128)(2,1)S(1)} all-reduce(bf16[128]{0:T(256)(128)(2,1)S(1)} %dynamic-update-slice), channel_id=2, replica_groups=mesh['dp'=4,'latent'=32] {'latent'}, use_global_device_ids=true, to_apply=%add | all-reduce | flops 128 | bytes 512
  97.7 0.0 all-gather.3.cloned.1.call-done
  97.8 7.3 %multiply_reduce_fusion = (f32[512]{0:T(512)S(1)}, f32[128,512]{1,0:T(8,128)S(1)}) fusion(f32[128]{0:T(128)S(1)} %mul.102, f32[512]{0:T(512)} %param.11, bf16[8192,512]{1,0:T(8,128)(2,1)} %bitcast.33, bf16[128,1,8192]{2,1,0:T(2,128)(2,1)} %all-gather.3.cloned.1.call-done), kind=kOutput, calls=%fused_computation.26 | convolution fusion | flops 1074068992 | bytes 10752512 | tf_op jit(solution)/shard_map/dot_general | solution.py:44
  105.1 6.0 %convolution_convert_fusion = bf16[128,8192]{1,0:T(8,128)(2,1)} fusion(bf16[512,8192]{1,0:T(8,128)(2,1)} %param.12, f32[128,512]{1,0:T(8,128)S(1)} %get-tuple-element.16), kind=kOutput, calls=%fused_computation.6 | convolution fusion | flops 1074921472 | bytes 10747904 | tf_op jit(solution)/shard_map/dot_general | solution.py:48
  111.0 0.0 all-reduce.4.cloned.1.call-update
  111.1 0.0 copy-start.2
  111.1 0.2 reduce-scatter.3.cloned.1.call-start
  111.3 11.3 %convert_multiply_fusion.1 = f32[512,8192]{1,0:T(8,128)} fusion(bf16[512,8192]{1,0:T(8,128)(2,1)} %param.12), kind=kLoop, calls=%fused_computation.3 | loop fusion | flops 8388608 | bytes 25165824 | tf_op jit(solution)/shard_map/square | solution.py:38
  122.6 0.0 copy-done.2
  122.6 6.5 %slice_reduce_fusion.1 = (f32[512]{0:T(512)S(1)}, f32[512]{0:T(512)S(1)}) fusion(f32[512,8192]{1,0:T(8,128)} %convert_multiply_fusion.1), kind=kLoop, calls=%fused_computation.8 | loop fusion | flops 4193280 | bytes 16781312 | tf_op jit(solution)/shard_map/reduce_sum | solution.py:39
  129.2 8.8 %copy.19 = bf16[128,1,8192]{0,2,1:T(8,128)(2,1)S(1)} copy(bf16[128,1,8192]{2,1,0:T(2,128)(2,1)} %all-gather.3.cloned.1.call-done) | data formatting | bytes 4194304 | tf_op jit(solution)/shard_map/dot_general | solution.py:61
  138.0 0.6 multiply_reduce_fusion.2
  138.6 75.9 %all-reduce.4.cloned.1.call-done = bf16[128,8192]{1,0:T(8,128)(2,1)} async-done(((bf16[128,8192]{1,0:T(8,128)(2,1)}), bf16[128,8192]{1,0:T(8,128)(2,1)}) %all-reduce.4.cloned.1.call-update) | async-done | bytes 2097168 | tf_op jit(solution)/shard_map/psum | solution.py:49
  214.5 8.7 %subtract_multiply_fusion = f32[128,8192]{1,0:T(8,128)} fusion(bf16[128,8192]{1,0:T(8,128)(2,1)} %all-reduce.4.cloned.1.call-done, f32[128]{0:T(128)S(1)} %mul.102, f32[8192]{0:T(1024)S(1)} %bitcast.36, bf16[128,1,8192]{2,1,0:T(2,128)(2,1)} %all-gather.3.cloned.1.call-done), kind=kLoop, calls=%fused_computation.12 | loop fusion | flops 5242880 | bytes 8421888 | tf_op jit(solution)/shard_map/mul | solution.py:50
  223.2 15.0 %convolution_convert_fusion.1 = bf16[2,4096,512]{2,1,0:T(8,128)(2,1)} fusion(bf16[2,4096,128]{2,1,0:T(8,128)(2,1)S(1)} %bitcast.34, f32[128,512]{1,0:T(8,128)S(1)} %get-tuple-element.16, bf16[512,8192]{1,0:T(8,128)(2,1)} %param.12, f32[128,8192]{1,0:T(8,128)} %subtract_multiply_fusion, f32[512]{0:T(512)S(1)} %get-tuple-element.10, f32[128]{0:T(128)S(1)} %mul.102), kind=kOutput, calls=%fused_computation.9 | convolution fusion | flops 2153119744 | bytes 23333376 | tf_op jit(solution)/shard_map/dot_general | solution.py:61
  238.2 0.0 reduce-scatter.3.cloned.1.call-update
  238.2 0.0 reduce-scatter.5.cloned.1.call-start
  238.3 9.8 %fusion.1 = bf16[512,8192]{1,0:T(8,128)(2,1)} fusion(bf16[512,8192]{1,0:T(8,128)(2,1)} %param.12, f32[512]{0:T(512)S(1)} %get-tuple-element.12, f32[512]{0:T(512)S(1)} %get-tuple-element.11, pred[8192]{0:T(1024)(128)(4,1)S(1)} %iota_compare_fusion, f32[128,8192]{1,0:T(8,128)} %subtract_multiply_fusion, f32[128,512]{1,0:T(8,128)S(1)} %get-tuple-element.16), kind=kOutput, calls=%fused_computation.5 | convolution fusion | flops 1100087296 | bytes 21245952 | tf_op jit(solution)/shard_map/dot_general | solution.py:65
  248.0 0.0 reduce-scatter.5.cloned.1.call-update
  248.1 1.6 multiply_reduce_fusion.1
  251.0 69.5 %all-reduce.1 = (f32[]{:T(128)}, f32[]{:T(128)}) all-reduce(f32[]{:T(128)} %get-tuple-element.13, f32[]{:T(128)S(6)} %add.86), channel_id=1, replica_groups=mesh['dp'=4,'latent'=32] {'dp','latent'}, use_global_device_ids=true, to_apply=%region_6.7 | all-reduce | flops 2 | bytes 16 | tf_op jit(solution)/shard_map/psum | solution.py:78
  321.8 0.0 copy-start.1
  322.5 0.0 reduce-scatter.3.cloned.1.call-done
  322.5 3.3 multiply_convert_fusion.1
  325.8 77.3 %reduce-scatter.5.cloned.1.call-done = bf16[512,2048]{1,0:T(8,128)(2,1)} async-done(((bf16[512,8192]{1,0:T(8,128)(2,1)}), bf16[512,2048]{1,0:T(8,128)(2,1)}) %reduce-scatter.5.cloned.1.call-update) | async-done | bytes 2097168 | tf_op jit(solution)/shard_map/reduce_scatter | solution.py:75
  403.2 3.4 multiply_convert_fusion
  406.6 0.0 copy-done.1
  (8 shorter events, 0.0 us)
Async XLA Ops:
  7.2 1.7 copy-start
  7.2 90.6 %all-gather.3.cloned.1.call-start = ((), (), s32[]{:S(2)}) async-start(), calls=%async_computation.4 | async-start | bytes 4325376 | tf_op jit(solution)/shard_map/all_gather | solution.py:29
  24.3 7.2 %all-to-all-start.1 = ((bf16[4,1,1]{2,1,0:T(2,128)(2,1)}), bf16[4,1,1]{2,1,0:T(2,128)(2,1)S(1)}, u32[]{:S(2)}, u32[]{:S(2)}) async-start(bf16[4,1,1]{2,1,0:T(2,128)(2,1)} %copy.17), calls=%async_computation.1 | async-start | bytes 4096 | tf_op jit(solution)/shard_map/all_to_all | solution.py:26
  27.5 187.0 %all-reduce.4.cloned.1.call-start = ((), (), s32[]{:S(2)}) async-start(), calls=%async_computation.5 | async-start | bytes 4194304 | tf_op jit(solution)/shard_map/psum | solution.py:49
  111.1 11.6 %copy-start.2 = (f32[2,4096]{1,0:T(2,128)S(1)}, f32[2,4096]{1,0:T(2,128)}, u32[]{:S(2)}) copy-start(f32[2,4096]{1,0:T(2,128)} %param.13) | copy-start | bytes 98308
  111.1 211.4 %reduce-scatter.3.cloned.1.call-start = ((), (), s32[]{:S(2)}) async-start(), calls=%async_computation.6 | async-start | bytes 10485760 | tf_op jit(solution)/shard_map/reduce_scatter | solution.py:72
  238.2 165.0 %reduce-scatter.5.cloned.1.call-start = ((), (), s32[]{:S(2)}) async-start(), calls=%async_computation.7 | async-start | bytes 10485760 | tf_op jit(solution)/shard_map/reduce_scatter | solution.py:75
  321.8 84.8 %copy-start.1 = (bf16[5,8192]{1,0:T(8,128)(2,1)S(1)}, bf16[5,8192]{1,0:T(8,128)(2,1)}, u32[]{:S(2)}) copy-start(bf16[5,8192]{1,0:T(8,128)(2,1)} %param.7) | copy-start | bytes 245764
Sparse Core Ops, SparseCore 0:
  21.8 47.3 all-gather.2
  111.2 103.2 all-reduce.3
  238.3 82.5 reduce-scatter.2
  323.2 79.8 reduce-scatter.4
where the time goes:
time: 415 us; the launch traced here: 414 us
  waiting for transfers between devices  155 us (37%)
  blocking collectives  145 us (35%)
  other arithmetic  38.6 us (9%)
  matrix products  38 us (9%)
  between operations  19.7 us (5%)
  local copies, waits for them, and re-layouts  13.6 us (3%)
    reduce_scatter x1, waiting for transfers between devices, shards(): lax.psum_scatter(dec_term.astype(jnp.bfloat16), 'dp', scatter_dimension=1...  77.3 us
    psum x1, waiting for transfers between devices, shards(): lax.psum(partial_value.astype(jnp.bfloat16), 'latent').astype(jnp.float32)  75.9 us
    psum x1, blocking collectives, shards(): total, count = lax.psum((local_loss, own_count), ('dp', 'latent'))  69.5 us
    unnamed x1, blocking collectives  65.9 us
    dot_general x1, matrix products, shards(): lax.dot_general(xg, dpre16, (((0,), (0,)), ((), ())), preferred_element_t...  15 us
    square x1, other arithmetic, shards(): squares_dec = jnp.square(w_dec.astype(jnp.float32))  11.3 us
    all_to_all x1, blocking collectives, shards(): lax.all_to_all(outgoing, 'dp', split_axis=0, concat_axis=0, tiled=True)  10.1 us
    dot_general x1, matrix products, shards(): lax.dot_general(feats16, err16, (((0,), (0,)), ((), ())), preferred_eleme...  9.77 us
  transfers between devices with their start and end apart: 5, of which 3 were waited for; matrix products, arithmetic and copies ran while one was open for 11% of the time, Pallas kernels for 0%

commit v1 on v0

--- a/solution.py
+++ b/solution.py
@@ -75,7 +75,7 @@
     dec_total = lax.psum_scatter(
         dec_term.astype(jnp.bfloat16), "dp", scatter_dimension=1, tiled=True
     ).astype(jnp.float32)
-    total, count = lax.psum((local_loss, own_count), ("dp", "latent"))
+    total, count = lax.psum(lax.psum((local_loss, own_count), axis_name="latent"), axis_name="dp")
     factor = loss_scale / count
     grad_enc = (enc_total * factor).astype(jnp.bfloat16)
     grad_dec = (dec_total * factor).astype(jnp.bfloat16)

time: 415 us -> 414 us (level)
    reduce_scatter x1, waiting for transfers between devices: 77.3 us -> 72.6 us  [shards(): lax.psum_scatter(dec_term.astype(jnp.bfloat16), 'dp', scatter_dimension=1...]
    psum x1 -> x2, blocking collectives: 69.5 us -> 72.7 us  [the longest x1 63.5 us: shards(): lax.psum((local_loss, own_count), axis_name='latent')]
where the time goes in v1:
time: 414 us; the launch traced here: 413 us
  waiting for transfers between devices  151 us (36%)
  blocking collectives  149 us (36%)
  other arithmetic  38.6 us (9%)
  matrix products  38 us (9%)
  between operations  19.7 us (5%)
  local copies, waits for them, and re-layouts  13.6 us (3%)
    psum x1, waiting for transfers between devices, shards(): lax.psum(partial_value.astype(jnp.bfloat16), 'latent').astype(jnp.float32)  75.9 us
    reduce_scatter x1, waiting for transfers between devices, shards(): lax.psum_scatter(dec_term.astype(jnp.bfloat16), 'dp', scatter_dimension=1...  72.6 us
    unnamed x1, blocking collectives  65.9 us
    psum x1, blocking collectives, shards(): lax.psum((local_loss, own_count), axis_name='latent')  63.5 us
    dot_general x1, matrix products, shards(): lax.dot_general(xg, dpre16, (((0,), (0,)), ((), ())), preferred_element_t...  15 us
    square x1, other arithmetic, shards(): squares_dec = jnp.square(w_dec.astype(jnp.float32))  11.3 us
    all_to_all x1, blocking collectives, shards(): lax.all_to_all(outgoing, 'dp', split_axis=0, concat_axis=0, tiled=True)  10.1 us
    dot_general x1, matrix products, shards(): lax.dot_general(feats16, err16, (((0,), (0,)), ((), ())), preferred_eleme...  9.77 us
  transfers between devices with their start and end apart: 5, of which 3 were waited for; matrix products, arithmetic and copies ran while one was open for 11% of the time, Pallas kernels for 0%

profile of v1, /device:TPU:1, one launch (start us, length us, event | category | flops | bytes accessed | tf_op | source)
XLA Modules:
  0.0 412.8 jit_solution(11487368720616788245)
XLA Ops:
  7.2 0.0 copy-start
  7.2 0.0 all-gather.3.cloned.1.call-start
  7.2 1.6 sort.17
  8.9 0.0 copy-done
  8.9 0.6 gather_fusion
  9.5 0.5 broadcast.57
  10.0 0.7 reduce.2
  10.7 0.1 reshape.95
  10.8 10.1 %all_to_all.14 = bf16[4,2,4096]{2,1,0:T(2,128)(2,1)S(1)} all-to-all(bf16[4,2,4096]{2,1,0:T(2,128)(2,1)S(1)} %reshape.95), channel_id=1, replica_groups=mesh['dp'=4,'latent'=32] {'dp'}, dimensions={0} | all-to-all | bytes 131072 | tf_op jit(solution)/shard_map/all_to_all | solution.py:25
  20.9 0.7 reshape.96
  21.6 0.0 all-gather.3.cloned.1.call-update
  22.3 0.6 gather_fusion.1
  23.0 0.6 fusion.25
  23.6 0.7 copy.17
  24.3 3.2 all-to-all-start.1
  27.5 0.0 all-reduce.5.cloned.1.call-start
  27.5 1.3 dynamic-slice
  29.6 1.9 all-to-all-done.1
  31.5 0.1 reduce.1
  31.6 0.2 dynamic-update-slice
  31.8 65.9 %all-reduce = bf16[128]{0:T(256)(128)(2,1)S(1)} all-reduce(bf16[128]{0:T(256)(128)(2,1)S(1)} %dynamic-update-slice), channel_id=2, replica_groups=mesh['dp'=4,'latent'=32] {'latent'}, use_global_device_ids=true, to_apply=%add | all-reduce | flops 128 | bytes 512
  97.7 0.0 all-gather.3.cloned.1.call-done
  97.8 7.3 %multiply_reduce_fusion = (f32[512]{0:T(512)S(1)}, f32[128,512]{1,0:T(8,128)S(1)}) fusion(f32[128]{0:T(128)S(1)} %mul.102, f32[512]{0:T(512)} %param.11, bf16[8192,512]{1,0:T(8,128)(2,1)} %bitcast.33, bf16[128,1,8192]{2,1,0:T(2,128)(2,1)} %all-gather.3.cloned.1.call-done), kind=kOutput, calls=%fused_computation.26 | convolution fusion | flops 1074068992 | bytes 10752512 | tf_op jit(solution)/shard_map/dot_general | solution.py:44
  105.1 6.0 %convolution_convert_fusion = bf16[128,8192]{1,0:T(8,128)(2,1)} fusion(bf16[512,8192]{1,0:T(8,128)(2,1)} %param.12, f32[128,512]{1,0:T(8,128)S(1)} %get-tuple-element.18), kind=kOutput, calls=%fused_computation.6 | convolution fusion | flops 1074921472 | bytes 10747904 | tf_op jit(solution)/shard_map/dot_general | solution.py:48
  111.0 0.0 all-reduce.5.cloned.1.call-update
  111.1 0.0 copy-start.2
  111.1 0.2 reduce-scatter.3.cloned.1.call-start
  111.3 11.3 %convert_multiply_fusion.1 = f32[512,8192]{1,0:T(8,128)} fusion(bf16[512,8192]{1,0:T(8,128)(2,1)} %param.12), kind=kLoop, calls=%fused_computation.3 | loop fusion | flops 8388608 | bytes 25165824 | tf_op jit(solution)/shard_map/square | solution.py:38
  122.6 0.0 copy-done.2
  122.6 6.5 %slice_reduce_fusion.1 = (f32[512]{0:T(512)S(1)}, f32[512]{0:T(512)S(1)}) fusion(f32[512,8192]{1,0:T(8,128)} %convert_multiply_fusion.1), kind=kLoop, calls=%fused_computation.8 | loop fusion | flops 4193280 | bytes 16781312 | tf_op jit(solution)/shard_map/reduce_sum | solution.py:39
  129.2 8.8 %copy.19 = bf16[128,1,8192]{0,2,1:T(8,128)(2,1)S(1)} copy(bf16[128,1,8192]{2,1,0:T(2,128)(2,1)} %all-gather.3.cloned.1.call-done) | data formatting | bytes 4194304 | tf_op jit(solution)/shard_map/dot_general | solution.py:61
  138.0 0.6 multiply_reduce_fusion.2
  138.6 75.9 %all-reduce.5.cloned.1.call-done = bf16[128,8192]{1,0:T(8,128)(2,1)} async-done(((bf16[128,8192]{1,0:T(8,128)(2,1)}), bf16[128,8192]{1,0:T(8,128)(2,1)}) %all-reduce.5.cloned.1.call-update) | async-done | bytes 2097168 | tf_op jit(solution)/shard_map/psum | solution.py:49
  214.5 8.7 %subtract_multiply_fusion = f32[128,8192]{1,0:T(8,128)} fusion(bf16[128,8192]{1,0:T(8,128)(2,1)} %all-reduce.5.cloned.1.call-done, f32[128]{0:T(128)S(1)} %mul.102, f32[8192]{0:T(1024)S(1)} %bitcast.36, bf16[128,1,8192]{2,1,0:T(2,128)(2,1)} %all-gather.3.cloned.1.call-done), kind=kLoop, calls=%fused_computation.12 | loop fusion | flops 5242880 | bytes 8421888 | tf_op jit(solution)/shard_map/mul | solution.py:50
  223.2 15.0 %convolution_convert_fusion.1 = bf16[2,4096,512]{2,1,0:T(8,128)(2,1)} fusion(bf16[2,4096,128]{2,1,0:T(8,128)(2,1)S(1)} %bitcast.34, f32[128,512]{1,0:T(8,128)S(1)} %get-tuple-element.18, bf16[512,8192]{1,0:T(8,128)(2,1)} %param.12, f32[128,8192]{1,0:T(8,128)} %subtract_multiply_fusion, f32[512]{0:T(512)S(1)} %get-tuple-element.12, f32[128]{0:T(128)S(1)} %mul.102), kind=kOutput, calls=%fused_computation.9 | convolution fusion | flops 2153119744 | bytes 23333376 | tf_op jit(solution)/shard_map/dot_general | solution.py:61
  238.2 0.0 reduce-scatter.3.cloned.1.call-update
  238.2 0.0 reduce-scatter.5.cloned.1.call-start
  238.3 9.8 %fusion.1 = bf16[512,8192]{1,0:T(8,128)(2,1)} fusion(bf16[512,8192]{1,0:T(8,128)(2,1)} %param.12, f32[512]{0:T(512)S(1)} %get-tuple-element.14, f32[512]{0:T(512)S(1)} %get-tuple-element.13, pred[8192]{0:T(1024)(128)(4,1)S(1)} %iota_compare_fusion, f32[128,8192]{1,0:T(8,128)} %subtract_multiply_fusion, f32[128,512]{1,0:T(8,128)S(1)} %get-tuple-element.18), kind=kOutput, calls=%fused_computation.5 | convolution fusion | flops 1100087296 | bytes 21245952 | tf_op jit(solution)/shard_map/dot_general | solution.py:65
  248.0 0.0 reduce-scatter.5.cloned.1.call-update
  248.1 1.6 multiply_reduce_fusion.1
  251.0 63.5 %all-reduce.1 = (f32[]{:T(128)}, f32[]{:T(128)}) all-reduce(f32[]{:T(128)} %get-tuple-element.15, f32[]{:T(128)S(6)} %add.90), channel_id=1, replica_groups=mesh['dp'=4,'latent'=32] {'latent'}, use_global_device_ids=true, to_apply=%region_6.7 | all-reduce | flops 2 | bytes 16 | tf_op jit(solution)/shard_map/psum | solution.py:78
  314.4 9.3 %all-reduce.2 = (f32[]{:T(128)}, f32[]{:T(128)}) all-reduce(f32[]{:T(128)} %get-tuple-element.7, f32[]{:T(128)} %get-tuple-element.8), channel_id=1, replica_groups=mesh['dp'=4,'latent'=32] {'dp'}, use_global_device_ids=true, to_apply=%region_7.8 | all-reduce | flops 2 | bytes 16 | tf_op jit(solution)/shard_map/psum | solution.py:78
  325.1 0.0 copy-start.1
  325.8 0.0 reduce-scatter.3.cloned.1.call-done
  325.8 3.3 multiply_convert_fusion.1
  329.1 72.6 %reduce-scatter.5.cloned.1.call-done = bf16[512,2048]{1,0:T(8,128)(2,1)} async-done(((bf16[512,8192]{1,0:T(8,128)(2,1)}), bf16[512,2048]{1,0:T(8,128)(2,1)}) %reduce-scatter.5.cloned.1.call-update) | async-done | bytes 2097168 | tf_op jit(solution)/shard_map/reduce_scatter | solution.py:75
  401.7 3.4 multiply_convert_fusion
  405.1 0.0 copy-done.1
  (8 shorter events, 0.0 us)
Async XLA Ops:
  7.2 1.7 copy-start
  7.2 90.6 %all-gather.3.cloned.1.call-start = ((), (), s32[]{:S(2)}) async-start(), calls=%async_computation.4 | async-start | bytes 4325376 | tf_op jit(solution)/shard_map/all_gather | solution.py:29
  24.3 7.2 %all-to-all-start.1 = ((bf16[4,1,1]{2,1,0:T(2,128)(2,1)}), bf16[4,1,1]{2,1,0:T(2,128)(2,1)S(1)}, u32[]{:S(2)}, u32[]{:S(2)}) async-start(bf16[4,1,1]{2,1,0:T(2,128)(2,1)} %copy.17), calls=%async_computation.1 | async-start | bytes 4096 | tf_op jit(solution)/shard_map/all_to_all | solution.py:26
  27.5 187.0 %all-reduce.5.cloned.1.call-start = ((), (), s32[]{:S(2)}) async-start(), calls=%async_computation.5 | async-start | bytes 4194304 | tf_op jit(solution)/shard_map/psum | solution.py:49
  111.1 11.6 %copy-start.2 = (f32[2,4096]{1,0:T(2,128)S(1)}, f32[2,4096]{1,0:T(2,128)}, u32[]{:S(2)}) copy-start(f32[2,4096]{1,0:T(2,128)} %param.13) | copy-start | bytes 98308
  111.1 214.7 %reduce-scatter.3.cloned.1.call-start = ((), (), s32[]{:S(2)}) async-start(), calls=%async_computation.6 | async-start | bytes 10485760 | tf_op jit(solution)/shard_map/reduce_scatter | solution.py:72
  238.2 163.5 %reduce-scatter.5.cloned.1.call-start = ((), (), s32[]{:S(2)}) async-start(), calls=%async_computation.7 | async-start | bytes 10485760 | tf_op jit(solution)/shard_map/reduce_scatter | solution.py:75
  325.1 80.1 %copy-start.1 = (bf16[5,8192]{1,0:T(8,128)(2,1)S(1)}, bf16[5,8192]{1,0:T(8,128)(2,1)}, u32[]{:S(2)}) copy-start(bf16[5,8192]{1,0:T(8,128)(2,1)} %param.7) | copy-start | bytes 245764
Sparse Core Ops, SparseCore 0:
  21.8 47.3 all-gather.2
  111.2 103.2 all-reduce.4
  238.3 80.6 reduce-scatter.2
  321.3 80.3 reduce-scatter.4
